TPU v7x, 32 devices: a whole 2x2x4 slice. The times are simulated.
32 devices in a mesh: tm: 8 (over z, x), chan: 4 (over y, core).
Axes of the slice: x: 2, y: 2, z: 4, core: 2. Of those that a mesh axis runs over, the one named last changes fastest.
Arguments:
- surveillance: bfloat16 [128, 1024, 256], P(('chan', 'tm')), parts along dimension 0, may hold values from -6 to 6
- ref_samples: bfloat16 [32, 1040, 256], P('tm'), may hold values from -6 to 6
- block_ids: int32 [32], P('tm'), may hold values from 0 to 31, each once
- walk: int32 [32], P('tm'), may hold values from 0 to 63
- cfar_guard: int32 [2048], P('tm'), may hold values from 1 to 8
- cfar_window: int32 [2048], P('tm'), may hold values from 1 to 16
Outputs:
- detection: float32 [8192, 512], P(('chan', 'tm')), parts along dimension 0
There are 4 independent parts, one for each index of `chan`. A program takes and returns all parts, laid end to end along the dimension named above; an argument that names none is the same for every part. Nothing has to cross between parts.
Inputs may be any that keep to these rules, and one draw needn't show every extreme that they name: block_ids names each of 0 to 31 exactly once.
All inputs are finite; a program needn't handle non-finite values.
Results may differ from a plain program's by a relative error of at most 0.0003.
Values sent between devices are 32-bit elements; how exact they have to be, the bound alone decides.
A program may use at most 64 MiB of HBM per device.

v0:
```python
import math

import jax
import jax.numpy as jnp
from jax import lax
from jax.sharding import PartitionSpec as P

D = 2048
DOP = 512
SEGS = 64
GUARD_MAX = 8
WIN_MAX = 16


HIGH = lax.Precision.HIGHEST


def with_halo(x, sides, width):
    for axis, dim in sides:
        count, length = (lax.axis_size(axis), x.shape[dim])
        up = [(i, (i + 1) % count) for i in range(count - 1)]
        down = [(j, i) for i, j in up]
        last = lax.slice_in_dim(x, length - width, length, axis=dim)
        initial = lax.slice_in_dim(x, 0, width, axis=dim)
        before = lax.ppermute(last, axis, up)
        after = lax.ppermute(initial, axis, down)
        x = jnp.concatenate([before, x, after], axis=dim)
    return x


def phase(product, total):
    return 2.0 * math.pi / total * (product % total).astype(jnp.float32)


def square_tables(width):
    place = jnp.arange(width, dtype=jnp.int32)
    theta = phase(place[:, None] * place[None, :], width)
    return (jnp.cos(theta), jnp.sin(theta))


def make_tables():
    length = 2 * D
    rows = length // 128
    small_cos, small_sin = square_tables(rows)
    wide_cos, wide_sin = square_tables(128)
    mixer = jnp.concatenate(
        [jnp.concatenate([wide_cos, -wide_sin], 1), jnp.concatenate([wide_sin, wide_cos], 1)], 0
    )
    first_idx = jnp.arange(rows, dtype=jnp.int32)[:, None]
    second_idx = jnp.arange(128, dtype=jnp.int32)[None, :]
    twist = phase(first_idx * second_idx, length)
    spread = first_idx + rows * second_idx
    return (small_cos, small_sin, jnp.cos(twist), jnp.sin(twist), mixer, spread)


def forward(signal, tables):
    small_cos, small_sin, twist_cos, twist_sin, mixer, spread = tables
    first = jnp.einsum("kn,snc->skc", small_cos, signal, precision=HIGH)
    second = jnp.einsum("kn,snc->skc", small_sin, signal, precision=HIGH)
    real_part = first[..., :128] + second[..., 128:]
    imag_part = first[..., 128:] - second[..., :128]
    turned = jnp.concatenate(
        [
            real_part * twist_cos + imag_part * twist_sin,
            imag_part * twist_cos - real_part * twist_sin,
        ],
        axis=-1,
    )
    return jnp.einsum("skc,cd->skd", turned, mixer, precision=HIGH)


def inverse(spectrum, tables):
    small_cos, small_sin, twist_cos, twist_sin, mixer, spread = tables
    mixed = jnp.dot(spectrum, mixer.T, precision=HIGH)
    real_part = mixed[:, :128]
    imag_part = mixed[:, 128:]
    turned = jnp.concatenate(
        [
            real_part * twist_cos - imag_part * twist_sin,
            imag_part * twist_cos + real_part * twist_sin,
        ],
        axis=-1,
    )
    with_cos = jnp.dot(small_cos, turned, precision=HIGH)
    with_sin = jnp.dot(small_sin, turned, precision=HIGH)
    result = jnp.concatenate(
        [with_cos[:, :128] - with_sin[:, 128:], with_cos[:, 128:] + with_sin[:, :128]], axis=-1
    )
    return result / (2.0 * D)


def correlate(surv_rows, ref_rows, shift, tables):
    seg_rows = D // 128
    rows_all = surv_rows.shape[0]
    segs = rows_all // seg_rows
    echo = surv_rows.astype(jnp.float32).reshape(segs, seg_rows, 256)
    echo = jnp.concatenate([echo, jnp.zeros_like(echo)], axis=1)
    direct = ref_rows.astype(jnp.float32)
    direct = jnp.concatenate(
        [
            direct[:rows_all].reshape(segs, seg_rows, 256),
            direct[seg_rows:].reshape(segs, seg_rows, 256),
        ],
        axis=1,
    )
    echo_hat = forward(echo, tables)
    direct_hat = forward(direct, tables)
    echo_re = echo_hat[..., :128]
    echo_im = echo_hat[..., 128:]
    direct_re = direct_hat[..., :128]
    direct_im = direct_hat[..., 128:]
    spec_re = jnp.sum(echo_re * direct_re + echo_im * direct_im, axis=0)
    spec_im = jnp.sum(echo_im * direct_re - echo_re * direct_im, axis=0)
    ramp = phase(tables[5] * shift, 2 * D)
    ramp_cos = jnp.cos(ramp)
    ramp_sin = jnp.sin(ramp)
    turned = jnp.concatenate(
        [spec_re * ramp_cos + spec_im * ramp_sin, spec_im * ramp_cos - spec_re * ramp_sin], axis=-1
    )
    lagged = inverse(turned, tables)
    picked = lagged[seg_rows:]
    delay_idx = (
        128 * jnp.arange(seg_rows, dtype=jnp.int32)[:, None]
        + (jnp.arange(256, dtype=jnp.int32) % 128)[None, :]
    )
    return jnp.where(delay_idx >= shift, picked, 0.0)


def doppler_mixer(ids, norm):
    freq = jnp.arange(DOP, dtype=jnp.int32)
    theta = phase(ids[:, None] * freq[None, :], DOP)
    cos_table = jnp.cos(theta) * norm
    sin_table = jnp.sin(theta) * norm
    return jnp.concatenate(
        [jnp.concatenate([cos_table, -sin_table], 1), jnp.concatenate([sin_table, cos_table], 1)], 0
    )


def body(surveillance, ref_samples, block_ids, walk, cfar_guard, cfar_window):
    blocks = surveillance.shape[0]
    devices = lax.axis_size("tm")
    total_blocks = blocks * devices
    span = D // devices
    reach = GUARD_MAX + WIN_MAX
    base = lax.axis_index("tm") * span
    tables = make_tables()
    corr = lax.map(
        lambda item: correlate(item[0], item[1], item[2], tables), (surveillance, ref_samples, walk)
    )
    real_c = corr[:, :, :128].reshape(blocks, D)
    imag_c = corr[:, :, 128:].reshape(blocks, D)
    norm = 1.0 / math.sqrt(total_blocks * SEGS * D)
    moved = lax.all_to_all(
        jnp.stack([real_c, imag_c], axis=1), "tm", split_axis=2, concat_axis=0, tiled=True
    )
    ids = lax.all_gather(block_ids, "tm", axis=0, tiled=True)
    stacked = jnp.concatenate([moved[:, 0], moved[:, 1]], 0)
    mixer = doppler_mixer(ids, norm)
    amp = lax.dot_general(stacked, mixer, (((0,), (0,)), ((), ())), precision=HIGH)
    floor = jnp.sum(moved * moved, axis=(0, 1))
    floor = floor / (total_blocks * SEGS * D)
    power = amp[:, :DOP] * amp[:, :DOP] + amp[:, DOP:] * amp[:, DOP:]
    padded = with_halo(power, (("tm", 0),), reach)
    guard = cfar_guard[:, None]
    width = cfar_window[:, None]

    def inside(dist):
        return ((dist > guard) & (dist <= guard + width)).astype(jnp.float32)

    row_idx = jnp.arange(span, dtype=jnp.int32)[:, None]
    col_idx = jnp.arange(span + 2 * reach, dtype=jnp.int32)[None, :]
    band = inside(jnp.abs(col_idx - reach - row_idx))
    spot = base + jnp.arange(span + 2 * reach, dtype=jnp.int32) - reach
    valid = ((spot >= 0) & (spot < D)).astype(jnp.float32)
    delay_sum = jnp.dot(band, padded, precision=HIGH)
    count = jnp.dot(band, valid, precision=HIGH)
    doppler_sum = jnp.zeros_like(power)
    for step in range(1, reach + 1):
        active = inside(jnp.full((1, 1), step, jnp.int32))
        doppler_sum = doppler_sum + active * (
            jnp.roll(power, -step, axis=1) + jnp.roll(power, step, axis=1)
        )
    noise = (delay_sum + doppler_sum) / (count[:, None] + 2.0 * width.astype(jnp.float32))
    return (power - floor[:, None]) / (0.25 + noise)


def solution(mesh):
    in_specs = (
        P(("chan", "tm"), None, None),
        P("tm", None, None),
        P("tm"),
        P("tm"),
        P("tm"),
        P("tm"),
    )
    out_specs = P(("chan", "tm"), None)
    return jax.shard_map(body, mesh=mesh, in_specs=in_specs, out_specs=out_specs, check_vma=False)
```

profile of v0, /device:TPU:0, one launch (start us, length us, event | category | flops | bytes accessed | tf_op | source)
XLA Modules:
  0.0 126.7 jit_solution(17962002947929078072)
XLA Ops:
  0.6 69.0 %while.15 = (s32[]{:T(128)}, f32[4,16,256]{2,1,0:T(8,128)S(1)}, s32[4]{0:T(128)}, bf16[4,1024,256]{2,1,0:T(8,128)(2,1)}, f32[256,256]{1,0:T(8,128)S(1)}, /*index...) while((s32[]{:T(128)}, f32[4,16,256]{2,1,0:T(8,128)S(1)}, s32[4]{0:T(128)}, ...), condition=%wide.region_3.4_spmd.clone.clone, body=%wide.region_0.3_spmd.clone.clone.sunk | while | flops 4067001856 | bytes 47000764 | solution.py:147
  0.6 1.3 %dynamic_slice.37 = s32[1]{0:T(128)} dynamic-slice(s32[4]{0:T(128)} %get-tuple-element.542, s32[]{:T(128)S(6)} %copy.37), dynamic_slice_sizes={1} | dynamic-slice | bytes 12 | tf_op jit(solution)/shard_map/while/body/jit(dynamic_index_in_dim)/dynamic_slice | solution.py:147
  2.0 1.1 constant_dynamic-slice_fusion.2
  3.1 1.1 dynamic-slice_convert_fusion.2
  4.4 2.0 %fusion.285 = f32[64,32,256]{2,1,0:T(8,128)S(1)} fusion(f32[64,16,256]{2,1,0:T(8,128)S(1)} %bitcast.89, f32[64,16,256]{2,1,0:T(8,128)S(1)} %bitcast.87), kind=kOutput, calls=%fused_computation.16.clone.1 | convolution fusion | flops 201865216 | bytes 4194304 | tf_op jit(solution)/shard_map/while/body/eval_jaxpr/kn,snc->skc/dot_general | solution.py:58
  6.4 2.0 %fusion.284 = f32[64,32,256]{2,1,0:T(8,128)S(1)} fusion(f32[64,16,256]{2,1,0:T(8,128)S(1)} %bitcast.90, f32[64,16,256]{2,1,0:T(8,128)S(1)} %bitcast.88), kind=kOutput, calls=%fused_computation.17.clone.1 | convolution fusion | flops 201865216 | bytes 4194304 | tf_op jit(solution)/shard_map/while/body/eval_jaxpr/kn,snc->skc/dot_general | solution.py:59
  8.4 1.0 convolution_bitcast_fusion.9
  9.5 1.0 convolution_bitcast_fusion.8
  11.3 1.9 %fusion.286 = f32[64,32,256]{2,1,0:T(8,128)S(1)} fusion(f32[64,32,128]{2,1,0:T(8,128)S(1)} %get-tuple-element.512, f32[64,32,128]{2,1,0:T(8,128)S(1)} %get-tuple-element.513, f32[256,256]{1,0:T(8,128)S(1)} %get-tuple-element.544), kind=kOutput, calls=%fused_computation.10.clone.1 | convolution fusion | flops 1611137024 | bytes 4456448 | tf_op jit(solution)/shard_map/while/body/eval_jaxpr/skc,cd->skd/dot_general | solution.py:69
  13.2 1.9 %fusion.287 = f32[64,32,256]{2,1,0:T(8,128)S(1)} fusion(f32[64,32,128]{2,1,0:T(8,128)S(1)} %get-tuple-element.514, f32[64,32,128]{2,1,0:T(8,128)S(1)} %get-tuple-element.515, f32[256,256]{1,0:T(8,128)S(1)} %get-tuple-element.544), kind=kOutput, calls=%fused_computation.5.clone.1 | convolution fusion | flops 1611137024 | bytes 4456448 | tf_op jit(solution)/shard_map/while/body/eval_jaxpr/skc,cd->skd/dot_general | solution.py:69
  17.8 1.3 %dynamic_slice.37 = s32[1]{0:T(128)} dynamic-slice(s32[4]{0:T(128)} %get-tuple-element.542, s32[]{:T(128)S(6)} %copy.37), dynamic_slice_sizes={1} | dynamic-slice | bytes 12 | tf_op jit(solution)/shard_map/while/body/jit(dynamic_index_in_dim)/dynamic_slice | solution.py:147
  19.2 1.1 constant_dynamic-slice_fusion.2
  20.3 1.1 dynamic-slice_convert_fusion.2
  21.6 2.0 %fusion.285 = f32[64,32,256]{2,1,0:T(8,128)S(1)} fusion(f32[64,16,256]{2,1,0:T(8,128)S(1)} %bitcast.89, f32[64,16,256]{2,1,0:T(8,128)S(1)} %bitcast.87), kind=kOutput, calls=%fused_computation.16.clone.1 | convolution fusion | flops 201865216 | bytes 4194304 | tf_op jit(solution)/shard_map/while/body/eval_jaxpr/kn,snc->skc/dot_general | solution.py:58
  23.6 2.0 %fusion.284 = f32[64,32,256]{2,1,0:T(8,128)S(1)} fusion(f32[64,16,256]{2,1,0:T(8,128)S(1)} %bitcast.90, f32[64,16,256]{2,1,0:T(8,128)S(1)} %bitcast.88), kind=kOutput, calls=%fused_computation.17.clone.1 | convolution fusion | flops 201865216 | bytes 4194304 | tf_op jit(solution)/shard_map/while/body/eval_jaxpr/kn,snc->skc/dot_general | solution.py:59
  25.7 1.0 convolution_bitcast_fusion.9
  26.7 1.0 convolution_bitcast_fusion.8
  28.5 1.9 %fusion.286 = f32[64,32,256]{2,1,0:T(8,128)S(1)} fusion(f32[64,32,128]{2,1,0:T(8,128)S(1)} %get-tuple-element.512, f32[64,32,128]{2,1,0:T(8,128)S(1)} %get-tuple-element.513, f32[256,256]{1,0:T(8,128)S(1)} %get-tuple-element.544), kind=kOutput, calls=%fused_computation.10.clone.1 | convolution fusion | flops 1611137024 | bytes 4456448 | tf_op jit(solution)/shard_map/while/body/eval_jaxpr/skc,cd->skd/dot_general | solution.py:69
  30.4 1.9 %fusion.287 = f32[64,32,256]{2,1,0:T(8,128)S(1)} fusion(f32[64,32,128]{2,1,0:T(8,128)S(1)} %get-tuple-element.514, f32[64,32,128]{2,1,0:T(8,128)S(1)} %get-tuple-element.515, f32[256,256]{1,0:T(8,128)S(1)} %get-tuple-element.544), kind=kOutput, calls=%fused_computation.5.clone.1 | convolution fusion | flops 1611137024 | bytes 4456448 | tf_op jit(solution)/shard_map/while/body/eval_jaxpr/skc,cd->skd/dot_general | solution.py:69
  35.1 1.3 %dynamic_slice.37 = s32[1]{0:T(128)} dynamic-slice(s32[4]{0:T(128)} %get-tuple-element.542, s32[]{:T(128)S(6)} %copy.37), dynamic_slice_sizes={1} | dynamic-slice | bytes 12 | tf_op jit(solution)/shard_map/while/body/jit(dynamic_index_in_dim)/dynamic_slice | solution.py:147
  36.5 1.1 constant_dynamic-slice_fusion.2
  37.6 1.1 dynamic-slice_convert_fusion.2
  38.9 2.0 %fusion.285 = f32[64,32,256]{2,1,0:T(8,128)S(1)} fusion(f32[64,16,256]{2,1,0:T(8,128)S(1)} %bitcast.89, f32[64,16,256]{2,1,0:T(8,128)S(1)} %bitcast.87), kind=kOutput, calls=%fused_computation.16.clone.1 | convolution fusion | flops 201865216 | bytes 4194304 | tf_op jit(solution)/shard_map/while/body/eval_jaxpr/kn,snc->skc/dot_general | solution.py:58
  40.9 2.0 %fusion.284 = f32[64,32,256]{2,1,0:T(8,128)S(1)} fusion(f32[64,16,256]{2,1,0:T(8,128)S(1)} %bitcast.90, f32[64,16,256]{2,1,0:T(8,128)S(1)} %bitcast.88), kind=kOutput, calls=%fused_computation.17.clone.1 | convolution fusion | flops 201865216 | bytes 4194304 | tf_op jit(solution)/shard_map/while/body/eval_jaxpr/kn,snc->skc/dot_general | solution.py:59
  42.9 1.0 convolution_bitcast_fusion.9
  43.9 1.0 convolution_bitcast_fusion.8
  45.8 1.9 %fusion.286 = f32[64,32,256]{2,1,0:T(8,128)S(1)} fusion(f32[64,32,128]{2,1,0:T(8,128)S(1)} %get-tuple-element.512, f32[64,32,128]{2,1,0:T(8,128)S(1)} %get-tuple-element.513, f32[256,256]{1,0:T(8,128)S(1)} %get-tuple-element.544), kind=kOutput, calls=%fused_computation.10.clone.1 | convolution fusion | flops 1611137024 | bytes 4456448 | tf_op jit(solution)/shard_map/while/body/eval_jaxpr/skc,cd->skd/dot_general | solution.py:69
  47.7 1.9 %fusion.287 = f32[64,32,256]{2,1,0:T(8,128)S(1)} fusion(f32[64,32,128]{2,1,0:T(8,128)S(1)} %get-tuple-element.514, f32[64,32,128]{2,1,0:T(8,128)S(1)} %get-tuple-element.515, f32[256,256]{1,0:T(8,128)S(1)} %get-tuple-element.544), kind=kOutput, calls=%fused_computation.5.clone.1 | convolution fusion | flops 1611137024 | bytes 4456448 | tf_op jit(solution)/shard_map/while/body/eval_jaxpr/skc,cd->skd/dot_general | solution.py:69
  52.3 1.3 %dynamic_slice.37 = s32[1]{0:T(128)} dynamic-slice(s32[4]{0:T(128)} %get-tuple-element.542, s32[]{:T(128)S(6)} %copy.37), dynamic_slice_sizes={1} | dynamic-slice | bytes 12 | tf_op jit(solution)/shard_map/while/body/jit(dynamic_index_in_dim)/dynamic_slice | solution.py:147
  53.7 1.1 constant_dynamic-slice_fusion.2
  54.8 1.1 dynamic-slice_convert_fusion.2
  56.1 2.0 %fusion.285 = f32[64,32,256]{2,1,0:T(8,128)S(1)} fusion(f32[64,16,256]{2,1,0:T(8,128)S(1)} %bitcast.89, f32[64,16,256]{2,1,0:T(8,128)S(1)} %bitcast.87), kind=kOutput, calls=%fused_computation.16.clone.1 | convolution fusion | flops 201865216 | bytes 4194304 | tf_op jit(solution)/shard_map/while/body/eval_jaxpr/kn,snc->skc/dot_general | solution.py:58
  58.1 2.0 %fusion.284 = f32[64,32,256]{2,1,0:T(8,128)S(1)} fusion(f32[64,16,256]{2,1,0:T(8,128)S(1)} %bitcast.90, f32[64,16,256]{2,1,0:T(8,128)S(1)} %bitcast.88), kind=kOutput, calls=%fused_computation.17.clone.1 | convolution fusion | flops 201865216 | bytes 4194304 | tf_op jit(solution)/shard_map/while/body/eval_jaxpr/kn,snc->skc/dot_general | solution.py:59
  60.1 1.0 convolution_bitcast_fusion.9
  61.2 1.0 convolution_bitcast_fusion.8
  63.0 1.9 %fusion.286 = f32[64,32,256]{2,1,0:T(8,128)S(1)} fusion(f32[64,32,128]{2,1,0:T(8,128)S(1)} %get-tuple-element.512, f32[64,32,128]{2,1,0:T(8,128)S(1)} %get-tuple-element.513, f32[256,256]{1,0:T(8,128)S(1)} %get-tuple-element.544), kind=kOutput, calls=%fused_computation.10.clone.1 | convolution fusion | flops 1611137024 | bytes 4456448 | tf_op jit(solution)/shard_map/while/body/eval_jaxpr/skc,cd->skd/dot_general | solution.py:69
  64.9 1.9 %fusion.287 = f32[64,32,256]{2,1,0:T(8,128)S(1)} fusion(f32[64,32,128]{2,1,0:T(8,128)S(1)} %get-tuple-element.514, f32[64,32,128]{2,1,0:T(8,128)S(1)} %get-tuple-element.515, f32[256,256]{1,0:T(8,128)S(1)} %get-tuple-element.544), kind=kOutput, calls=%fused_computation.5.clone.1 | convolution fusion | flops 1611137024 | bytes 4456448 | tf_op jit(solution)/shard_map/while/body/eval_jaxpr/skc,cd->skd/dot_general | solution.py:69
  69.7 1.3 %copy.22 = f32[4,2,2048]{0,1,2:T(2,128)S(1)} copy(f32[4,2,2048]{2,0,1:T(4,128)S(1)} %pad_maximum_fusion.11) | data formatting | bytes 131072 | tf_op jit(solution)/shard_map/stack | solution.py:154
  71.0 3.8 %reshape.198 = f32[8,1,2048]{2,1,0:T(1,128)} reshape(f32[2048,2,4]{2,1,0:T(2,128)S(1)} %bitcast.93) | data formatting | bytes 131072
  74.8 7.3 %all-to-all-start = ((f32[8,1,2048]{2,1,0:T(1,128)}), f32[8,1,2048]{2,1,0:T(1,128)S(1)}, u32[]{:S(2)}, u32[]{:S(2)}) async-start(f32[8,1,2048]{2,1,0:T(1,128)} %reshape.198), calls=%async_computation | async-start | bytes 131072 | tf_op jit(solution)/shard_map/all_to_all | solution.py:153
  83.7 11.9 %all-reduce.1 = s32[32]{0:T(128)S(1)} all-reduce(s32[32]{0:T(128)S(1)} %dynamic-update-slice), channel_id=1, replica_groups=mesh['tm'=8,'chan'=4] {'tm'}, use_global_device_ids=true, to_apply=%add.1 | all-reduce | flops 32 | bytes 256
  97.6 3.2 %reshape.199 = f32[2048,2,4]{2,1,0:T(2,128)S(1)} reshape(f32[8,2048]{1,0:T(8,128)S(1)} %reduce.1) | data formatting | bytes 131072
  100.8 0.8 copy.26
  101.8 1.0 fusion.157
  110.6 3.4 %collective-permute-start = (f32[24,512]{1,0:T(8,128)S(1)}, f32[24,512]{1,0:T(8,128)S(1)}, u32[]{:S(2)}, u32[]{:S(2)}) collective-permute-start(f32[24,512]{1,0:T(8,128)S(1)} %get-tuple-element.415), channel_id=1, source_target_pairs={{0,4},{4,8},{8,12},{12,16},{16,20},{20,24},{24,28},{1,5},{5,9},{9,... | collective-permute-start | bytes 147464 | tf_op jit(solution)/shard_map/ppermute | solution.py:25
  114.0 1.5 %collective-permute-start.1 = (f32[24,512]{1,0:T(8,128)S(1)}, f32[24,512]{1,0:T(8,128)S(1)}, u32[]{:S(2)}, u32[]{:S(2)}) collective-permute-start(f32[24,512]{1,0:T(8,128)S(1)} %get-tuple-element.416), channel_id=1, source_target_pairs={{4,0},{8,4},{12,8},{16,12},{20,16},{24,20},{28,24},{5,1},{9,5},{13... | collective-permute-start | bytes 147464 | tf_op jit(solution)/shard_map/ppermute | solution.py:26
  115.7 4.3 %collective-permute-done.1 = f32[24,512]{1,0:T(8,128)S(1)} collective-permute-done((f32[24,512]{1,0:T(8,128)S(1)}, f32[24,512]{1,0:T(8,128)S(1)}, u32[]{:S(2)}, u32[]{:S(2)}) %collective-permute-start.1) | collective-permute-done | bytes 49184 | tf_op jit(solution)/shard_map/ppermute | solution.py:26
  120.0 6.7 %fusion.100 = f32[256,512]{1,0:T(8,128)} fusion(f32[24,512]{1,0:T(8,128)S(1)} %collective-permute-done.1, f32[256,512]{1,0:T(8,128)S(1)} %fusion.106, f32[24,512]{1,0:T(8,128)S(1)} %collective-permute-done, f32[256,1]{1,0:T(8,128)S(1)} %get-tuple-element.412, f32[256,511]{1,0:T(8,128)S(1)} %get-tuple-element.414, f32[256,511]{1,0:T(8,128)S(1)} %get-tuple-element.413, ...), kind=kOutput, calls=%fused_computation.128 | convolution fusion | flops 495104000 | bytes 26342592 | tf_op jit(solution)/shard_map/dot_general | solution.py:175
  (140 shorter events, 26.3 us)
Async XLA Ops:
  69.6 12.4 %copy-start.3 = (u32[32]{0:T(128)S(1)}, u32[32]{0:T(128)}, u32[]{:S(2)}) copy-start(u32[32]{0:T(128)} %constant.235) | copy-start | bytes 388
  69.7 13.8 %copy-start.2 = (s32[4]{0:T(128)S(1)}, s32[4]{0:T(128)}, u32[]{:S(2)}) copy-start(s32[4]{0:T(128)} %param.10) | copy-start | bytes 52
  69.7 25.9 %copy-start = (s32[256]{0:T(256)S(1)}, s32[256]{0:T(256)}, u32[]{:S(2)}) copy-start(s32[256]{0:T(256)} %param.12) | copy-start | bytes 3076
  69.7 25.9 %copy-start.1 = (s32[256]{0:T(256)S(1)}, s32[256]{0:T(256)}, u32[]{:S(2)}) copy-start(s32[256]{0:T(256)} %param.13) | copy-start | bytes 3076
  74.8 21.5 %all-to-all-start = ((f32[8,1,2048]{2,1,0:T(1,128)}), f32[8,1,2048]{2,1,0:T(1,128)S(1)}, u32[]{:S(2)}, u32[]{:S(2)}) async-start(f32[8,1,2048]{2,1,0:T(1,128)} %reshape.198), calls=%async_computation | async-start | bytes 131072 | tf_op jit(solution)/shard_map/all_to_all | solution.py:153
  110.6 5.1 %collective-permute-start = (f32[24,512]{1,0:T(8,128)S(1)}, f32[24,512]{1,0:T(8,128)S(1)}, u32[]{:S(2)}, u32[]{:S(2)}) collective-permute-start(f32[24,512]{1,0:T(8,128)S(1)} %get-tuple-element.415), channel_id=1, source_target_pairs={{0,4},{4,8},{8,12},{12,16},{16,20},{20,24},{24,28},{1,5},{5,9},{9,... | collective-permute-start | bytes 147464 | tf_op jit(solution)/shard_map/ppermute | solution.py:25
  114.0 6.0 %collective-permute-start.1 = (f32[24,512]{1,0:T(8,128)S(1)}, f32[24,512]{1,0:T(8,128)S(1)}, u32[]{:S(2)}, u32[]{:S(2)}) collective-permute-start(f32[24,512]{1,0:T(8,128)S(1)} %get-tuple-element.416), channel_id=1, source_target_pairs={{4,0},{8,4},{12,8},{16,12},{20,16},{24,20},{28,24},{5,1},{9,5},{13... | collective-permute-start | bytes 147464 | tf_op jit(solution)/shard_map/ppermute | solution.py:26
where the time goes:
time: 127 us
  matrix products  50.9 us (40%)
  local copies, waits for them, and re-layouts  28.4 us (22%)
  other arithmetic  17.3 us (14%)
  starting transfers between devices  12.2 us (10%)
  blocking collectives  11.9 us (9%)
  waiting for transfers between devices  4.46 us (4%)
    dot_general x8, matrix products, forward(): return jnp.einsum('skc,cd->skd', turned, mixer, precision=HIGH)  15.2 us
    dot_general x8, matrix products, forward(): second = jnp.einsum('kn,snc->skc', small_sin, signal, precision=HIGH)  12.2 us
    dot_general x8, matrix products, forward(): first = jnp.einsum('kn,snc->skc', small_cos, signal, precision=HIGH)  12.2 us
    unnamed x1, blocking collectives  11.9 us
    dynamic_slice x8, local copies, waits for them, and re-layouts, body(): lax.map(lambda item: correlate(item[0], item[1], item[2], tables), (surve...  9.53 us
    unnamed x15, local copies, waits for them, and re-layouts  7.96 us
    slice x48, local copies, waits for them, and re-layouts, body(): jnp.roll(power, step, axis=1)  7.45 us
    all_to_all x1, starting transfers between devices, body(): lax.all_to_all(jnp.stack([real_c, imag_c], axis=1), 'tm', split_axis=2, c...  7.27 us
  transfers between devices with their start and end apart: 3, of which 2 were waited for; matrix products, arithmetic and copies ran while one was open for 1% of the time, Pallas kernels for 0%

commit v1 on v0

v1 whole, which is shorter than its diff:
```python
import functools
import math

import numpy as np
import jax
import jax.numpy as jnp
from jax import lax
from jax.experimental import pallas as pl
from jax.experimental.pallas import tpu as pltpu
from jax.sharding import PartitionSpec as P

D = 2048
DOP = 512
SEGS = 64
GUARD_MAX = 8
WIN_MAX = 16
REACH = GUARD_MAX + WIN_MAX
LANES = 128
SEG_ROWS = D // LANES
CHUNK = SEG_ROWS * SEG_ROWS
MESH = pl.DeviceIdType.MESH
F32 = jnp.float32
BF16 = jnp.bfloat16


def window_rows(span):
    starts = range(0, D, span)
    return max((s + span + REACH - 1) // LANES - (s - REACH) // LANES + 1 for s in starts)


def iota(shape, dim):
    return lax.broadcasted_iota(jnp.int32, shape, dim)


def split(x):
    high = x.astype(BF16)
    return high, (x - high.astype(F32)).astype(BF16)


def mm(a, b, dims=((1,), (0,))):
    return lax.dot_general(a, b, (dims, ((), ())), preferred_element_type=F32)


def mm3(a, high, low):
    a_high, a_low = split(a)
    return mm(a_high, high) + (mm(a_low, high) + mm(a_high, low))


def correlate_kernel(span, walk_ref, ids_ref, s_ref, e_ref, out_ref, lhs_ref, rhs_ref, diag_ref, prev_ref):
    block = pl.program_id(0)
    chunks = s_ref.shape[1] // CHUNK
    devices, rows_sent = out_ref.shape[0], out_ref.shape[1] - 1
    blocks = out_ref.shape[2] // 2

    @pl.when(block == 0)
    def _():
        out_ref[...] = jnp.zeros_like(out_ref)
        ids = jnp.concatenate(
            [jnp.full((2, LANES), ids_ref[j], jnp.int32) for j in range(blocks)], 0
        ).astype(F32)
        for dev in range(devices):
            out_ref[dev, rows_sent] = ids

    q, row = iota((CHUNK, CHUNK), 0), iota((CHUNK, CHUNK), 1)
    swap = jnp.where(row == (q % SEG_ROWS) * SEG_ROWS + q // SEG_ROWS, 1.0, 0.0).astype(BF16)
    for ch in range(chunks):
        at = ch * CHUNK
        turned = mm(s_ref[0, at : at + CHUNK, :], swap, ((0,), (0,)))
        lhs_ref[:, at : at + CHUNK] = turned.astype(BF16)
        rhs_ref[ch, :CHUNK, :] = mm(swap, e_ref[0, at : at + CHUNK, :]).astype(BF16)
        late = at + SEG_ROWS
        rhs_ref[ch, CHUNK:, :] = mm(swap, e_ref[0, late : late + CHUNK, :]).astype(BF16)

    def product(a):
        off = pl.multiple_of((SEG_ROWS - a) * SEG_ROWS, SEG_ROWS)
        rhs = jnp.concatenate([rhs_ref[ch, pl.ds(off, CHUNK), :] for ch in range(chunks)], 0)
        g = mm(lhs_ref[...], rhs)
        return (
            g[:LANES, :LANES] + g[LANES:, LANES:],
            g[LANES:, :LANES] - g[:LANES, LANES:],
        )

    lower = iota((LANES, LANES), 1) <= iota((LANES, LANES), 0)
    prev_ref[0], prev_ref[1] = product(SEG_ROWS)
    group = 4

    def step(i, carry):
        later = [prev_ref[0], prev_ref[1]]
        for u in range(group):
            a = SEG_ROWS - 1 - (i * group + u)
            here = product(a)
            for part in range(2):
                x = jnp.where(lower, here[part], later[part])
                half = LANES // 2
                while half >= 8:
                    x = x[:half] + pltpu.roll(x[half:], LANES - half, 1)
                    half //= 2
                diag_ref[part, a] = x
            later = here
        prev_ref[0], prev_ref[1] = later
        return carry

    lax.fori_loop(0, SEG_ROWS // group, step, 0)

    x = diag_ref[...].reshape(2 * SEG_ROWS * 8, LANES)
    sub = iota(x.shape, 0) % 8
    for bit in (4, 2, 1):
        x = jnp.where((sub & bit) != 0, pltpu.roll(x, LANES - bit, 1), x)
    x = jnp.sum(x.reshape(2 * SEG_ROWS, 8, LANES), axis=1)
    shift = walk_ref[block]
    place = iota((LANES, LANES), 0) + iota((LANES, LANES), 1) - shift
    turn = jnp.where(place % LANES == 0, 1.0, 0.0).astype(BF16)
    high, rest = x.astype(BF16), None
    rest = x - high.astype(F32)
    mid, low = split(rest)
    x = mm(high, turn) + (mm(mid, turn) + mm(low, turn))
    before = iota((SEG_ROWS, LANES), 1) < shift
    for part in range(2):
        own = x[part * SEG_ROWS : (part + 1) * SEG_ROWS]
        above = jnp.concatenate([jnp.zeros((1, LANES), F32), own[: SEG_ROWS - 1]], 0)
        own = jnp.where(before, above, own)
        slot = 2 * block + part
        for dev in range(devices):
            first = (dev * span - REACH) // LANES
            for r in range(rows_sent):
                if 0 <= first + r < SEG_ROWS:
                    out_ref[dev, r, pl.ds(slot, 1), :] = own[first + r : first + r + 1]


def cosine(count):
    wrapped = (count + DOP // 2) % DOP - DOP // 2
    z = (DOP // 4 - jnp.abs(wrapped)).astype(F32) * (2.0 * math.pi / DOP)
    z2 = z * z
    poly = -1.0 / 39916800.0
    for c in (1.0 / 362880.0, -1.0 / 5040.0, 1.0 / 120.0, -1.0 / 6.0, 1.0):
        poly = poly * z2 + c
    return z * poly


def map_kernel(
    devices, span, send_ref, cfar_ref, dft_high, dft_low, tab_high, tab_low, ker_high, ker_low,
    out_ref, got, power_ref, coef_ref, send_sem, recv_sem,
):
    me = lax.axis_index("tm")
    rows_sent = send_ref.shape[1] - 1
    per = send_ref.shape[2]
    total = devices * per // 2
    barrier = pltpu.get_barrier_semaphore()
    peers = [lax.rem(me + k, devices) for k in range(1, devices)]
    for peer in peers:
        pl.semaphore_signal(barrier, inc=1, device_id={"tm": peer}, device_id_type=MESH)
    pl.semaphore_wait(barrier, devices - 1)
    copies = []
    for k, peer in enumerate(peers):
        copy = pltpu.make_async_remote_copy(
            src_ref=send_ref.at[peer],
            dst_ref=got.at[me],
            send_sem=send_sem.at[k],
            recv_sem=recv_sem.at[k],
            device_id={"tm": peer},
            device_id_type=MESH,
        )
        copy.start()
        copies.append(copy)
    got[me] = send_ref[me]

    width_all = rows_sent * LANES
    if span % LANES == 0:
        crop, lead = LANES - 32, 32
        width = span + 64
    else:
        crop, width = 0, width_all
        base = me * span - REACH + 2 * LANES
        lead = pl.multiple_of(base % LANES + REACH, 8)
    guard = cfar_ref[0:1, :].astype(F32)
    size = cfar_ref[1:2, :].astype(F32)
    guard = jnp.transpose(jnp.broadcast_to(guard, (LANES, span)))
    outer = guard + jnp.transpose(jnp.broadcast_to(size, (LANES, span)))
    dist = iota((span, LANES), 1).astype(F32)
    inside = jnp.where((dist > guard) & (dist <= outer), 1.0, 0.0).astype(BF16)
    kernel = mm(inside, ker_high[...]) + mm(inside, ker_low[...])
    guard, outer = guard[:, :1], outer[:, :1]
    dist = jnp.abs(iota((span, width), 1) - lead - iota((span, width), 0)).astype(F32)
    band = jnp.where((dist > guard) & (dist <= outer), 1.0, 0.0).astype(BF16)
    spot = (me * span + iota((span, 1), 0)).astype(F32)
    last = (D - 1) - spot
    count = jnp.minimum(spot, outer) - jnp.minimum(spot, guard)
    count = count + jnp.minimum(last, outer) - jnp.minimum(last, guard)
    weight = 1.0 / (count + 2.0 * (outer - guard))

    for copy in copies:
        copy.wait()
    stacked = jnp.concatenate(
        [
            jnp.concatenate([got[dev, r] for r in range(rows_sent)], 1)
            for dev in range(devices)
        ],
        0,
    )
    ids = jnp.concatenate([got[dev, rows_sent] for dev in range(devices)], 0)
    ids = ids[:, :1].astype(jnp.int32)
    shape = (devices * per, DOP)
    turns = ids * iota(shape, 1) - (DOP // 4) * (iota(shape, 0) % 2)
    mix_re_high, mix_re_low = split(cosine(turns))
    mix_im_high, mix_im_low = split(cosine(turns + DOP // 4))
    corr = jnp.transpose(stacked)[crop : crop + width]
    corr_high, corr_low = split(corr)
    norm = 1.0 / (total * SEGS * D)
    re = mm(corr_high, mix_re_high) + (mm(corr_low, mix_re_high) + mm(corr_high, mix_re_low))
    im = mm(corr_high, mix_im_high) + (mm(corr_low, mix_im_high) + mm(corr_high, mix_im_low))
    power = (re * re + im * im) * norm
    floor = jnp.sum(corr * corr, axis=1, keepdims=True) * norm
    coef = mm3(power, dft_high[...], dft_low[...])
    if span % LANES == 0:
        power_c = power[lead : lead + span]
        coef_c = coef[lead : lead + span]
        floor_c = floor[lead : lead + span]
    else:
        power_ref[:, :DOP] = power
        power_ref[:, DOP:] = jnp.broadcast_to(floor, (width, LANES))
        coef_ref[...] = coef
        power_c = power_ref[pl.ds(lead, span), :DOP]
        floor_c = power_ref[pl.ds(lead, span), DOP:][:, :1]
        coef_c = coef_ref[pl.ds(lead, span), :]
    coef_high, coef_low = split(coef)
    sums = mm(band, coef_high) + mm(band, coef_low) + coef_c * kernel
    noise = mm3(sums, tab_high[...], tab_low[...]) * weight
    out_ref[...] = (power_c - floor_c) / (0.25 + noise)


def np_split(x):
    high = x.astype(BF16)
    return jnp.asarray(high), jnp.asarray((x - high.astype(np.float64)).astype(BF16))


def tables(total):
    lag, freq = np.arange(total), np.arange(DOP)
    angle = 2.0 * np.pi / DOP * ((lag[:, None] * freq[None, :]) % DOP)
    tab = np.concatenate([np.cos(angle), np.sin(angle)], 0)
    scale = np.where(lag == 0, 1.0, 2.0) / DOP
    dft = tab.T * np.concatenate([scale, scale])[None, :]
    dist = np.arange(LANES)
    ker = 2.0 * np.cos(2.0 * np.pi / DOP * ((dist[:, None] * lag[None, :]) % DOP))
    ker = np.concatenate([ker, ker], 1)
    return (*np_split(dft), *np_split(tab), *np_split(ker))


def body(surveillance, ref_samples, block_ids, walk, cfar_guard, cfar_window):
    blocks, rows_all = surveillance.shape[:2]
    devices = lax.axis_size("tm")
    total = blocks * devices
    span = D // devices
    rows_sent = window_rows(span)
    chunks = rows_all // CHUNK
    send_shape = (devices, rows_sent + 1, 2 * blocks, LANES)
    smem = pl.BlockSpec(memory_space=pltpu.SMEM)
    vmem = pl.BlockSpec(memory_space=pltpu.VMEM)
    windows = pl.pallas_call(
        functools.partial(correlate_kernel, span),
        grid=(blocks,),
        out_shape=jax.ShapeDtypeStruct(send_shape, F32),
        in_specs=[
            smem,
            smem,
            pl.BlockSpec((1,) + surveillance.shape[1:], lambda j: (j, 0, 0)),
            pl.BlockSpec((1,) + ref_samples.shape[1:], lambda j: (j, 0, 0)),
        ],
        out_specs=pl.BlockSpec(send_shape, lambda j: (0, 0, 0, 0)),
        scratch_shapes=[
            pltpu.VMEM((2 * LANES, rows_all), BF16),
            pltpu.VMEM((chunks, 2 * CHUNK, 2 * LANES), BF16),
            pltpu.VMEM((2, SEG_ROWS, 8, LANES), F32),
            pltpu.VMEM((2, LANES, LANES), F32),
        ],
        compiler_params=pltpu.CompilerParams(dimension_semantics=("arbitrary",)),
        name="correlate",
    )(walk, block_ids, surveillance, ref_samples)
    width = span + 64 if span % LANES == 0 else rows_sent * LANES
    cfar = jnp.stack([cfar_guard, cfar_window])
    consts = tables(total)
    return pl.pallas_call(
        functools.partial(map_kernel, devices, span),
        out_shape=jax.ShapeDtypeStruct((span, DOP), F32),
        in_specs=[vmem] * 8,
        out_specs=vmem,
        scratch_shapes=[
            pltpu.VMEM(send_shape, F32),
            pltpu.VMEM((width, DOP + LANES), F32),
            pltpu.VMEM((width, 2 * total), F32),
            pltpu.SemaphoreType.DMA((devices,)),
            pltpu.SemaphoreType.DMA((devices,)),
        ],
        compiler_params=pltpu.CompilerParams(collective_id=0, has_side_effects=True),
        name="map",
    )(windows, cfar, *consts)


def solution(mesh):
    in_specs = (
        P(("chan", "tm"), None, None),
        P("tm", None, None),
        P("tm"),
        P("tm"),
        P("tm"),
        P("tm"),
    )
    out_specs = P(("chan", "tm"), None)
    return jax.shard_map(body, mesh=mesh, in_specs=in_specs, out_specs=out_specs, check_vma=False)
```

time: 127 us -> 41.8 us (0.33)
  matrix products: 50.9 us -> 0 us
  Pallas kernels: 0 us -> 38.4 us
  local copies, waits for them, and re-layouts: 28.4 us -> 1.87 us
  other arithmetic: 17.3 us -> 1.29 us
  starting transfers between devices: 12.2 us -> 0 us
  blocking collectives: 11.9 us -> 0 us
  waiting for transfers between devices: 4.46 us -> 0 us
    dot_general x39 -> x0, matrix products: 50.9 us -> none  [the longest x8 15.2 us: forward(): return jnp.einsum('skc,cd->skd', turned, mixer, precision=HIGH)]
    pallas_call x0 -> x2, Pallas kernels: none -> 38.4 us  [the longest x1 24.6 us: body(): pl.pallas_call(functools.partial(correlate_kernel, span), grid=(blocks,),...]
    unnamed x1 -> x0, blocking collectives: 11.9 us -> none
    dynamic_slice x8 -> x0, local copies, waits for them, and re-layouts: 9.53 us -> none  [body(): lax.map(lambda item: correlate(item[0], item[1], item[2], tables), (surve...]
    slice x55 -> x0, local copies, waits for them, and re-layouts: 8.18 us -> none  [the longest x48 7.45 us: body(): jnp.roll(power, step, axis=1)]
    all_to_all x1 -> x0, starting transfers between devices: 7.27 us -> none  [body(): lax.all_to_all(jnp.stack([real_c, imag_c], axis=1), 'tm', split_axis=2, c...]
    add x10 -> x0, other arithmetic: 6.21 us -> none  [the longest x4 3.06 us: forward(): real_part * twist_cos + imag_part * twist_sin]
    unnamed x15 -> x1, local copies, waits for them, and re-layouts: 7.96 us -> 1.87 us
  transfers between devices with their start and end apart: 3 -> 0, of which waited for: 2 -> 0; matrix products, arithmetic and copies ran while one was open for 1% -> 0% of each run, Pallas kernels for 0% -> 0%
where the time goes in v1:
time: 41.8 us; the launch traced here: 41.6 us
  Pallas kernels  38.4 us (92%)
  local copies, waits for them, and re-layouts  1.87 us (4%)
  other arithmetic  1.29 us (3%)
    pallas_call x1, Pallas kernels, body(): pl.pallas_call(functools.partial(correlate_kernel, span), grid=(blocks,),...  24.6 us
    pallas_call x1, Pallas kernels, body(): pl.pallas_call(functools.partial(map_kernel, devices, span), out_shape=ja...  13.8 us
    unnamed x1, local copies, waits for them, and re-layouts  1.87 us
    another operation x1, other arithmetic, body(): cfar = jnp.stack([cfar_guard, cfar_window])  1.29 us

profile of v1, /device:TPU:0, one launch (start us, length us, event | category | flops | bytes accessed | tf_op | source)
XLA Modules:
  0.0 41.6 jit_solution(8876736860591205849)
XLA Ops:
  0.0 1.3 %pad_add_fusion.cfar_ref = s32[2,256]{1,0:T(2,128)} fusion(s32[1,256]{1,0:T(1,128)} %bitcast.2, s32[1,256]{1,0:T(1,128)} %bitcast.3), kind=kLoop, calls=%fused_computation | loop fusion | flops 512 | bytes 4096 | tf_op jit(solution)/shard_map/stack | solution.py:279
  1.3 24.6 %correlate.1.send_ref = f32[8,5,8,128]{3,2,1,0:T(8,128)} custom-call(s32[4]{0:T(128)} %walk_ref.1, s32[4]{0:T(128)} %ids_ref.1, bf16[4,1024,256]{2,1,0:T(8,128)(2,1)} %s_ref.1, bf16[4,1040,256]{2,1,0:T(8,128)(2,1)} %e_ref.1), custom_call_target="tpu_custom_call" | custom-call | tf_op jit(solution)/shard_map/correlate/pallas_call | solution.py:258
  25.9 13.8 %map.1 = f32[256,512]{1,0:T(8,128)} custom-call(f32[8,5,8,128]{3,2,1,0:T(8,128)} %correlate.1.send_ref, s32[2,256]{1,0:T(2,128)} %pad_add_fusion.cfar_ref, bf16[512,64]{1,0:T(8,128)(2,1)} %constant.12.clone.dft_high, bf16[512,64]{1,0:T(8,128)(2,1)} %constant.13.clone.dft_low, bf16[64,512]{1,0:T(8,128)(2,1)} %constant.14.clone.tab_high, ...), custom_call_target="tpu_custom_call" | custom-call | tf_op jit(solution)/shard_map/map/pallas_call | solution.py:281
  39.7 1.9 %copy.14 = f32[256,512]{1,0:T(8,128)} copy(f32[256,512]{1,0:T(8,128)} %map.1) | data formatting | bytes 1048576

commit v2 on v1

v2 whole, which is shorter than its diff:
```python
import functools
import math

import numpy as np
import jax
import jax.numpy as jnp
from jax import lax
from jax.experimental import pallas as pl
from jax.experimental.pallas import tpu as pltpu
from jax.sharding import PartitionSpec as P

D = 2048
DOP = 512
SEGS = 64
GUARD_MAX = 8
WIN_MAX = 16
REACH = GUARD_MAX + WIN_MAX
LANES = 128
SEG_ROWS = D // LANES
CHUNK = SEG_ROWS * SEG_ROWS
MESH = pl.DeviceIdType.MESH
F32 = jnp.float32
BF16 = jnp.bfloat16


def window_rows(span):
    return max(s % LANES + span + 2 * REACH for s in range(0, D, span)) // LANES + 1


def iota(shape, dim):
    return lax.broadcasted_iota(jnp.int32, shape, dim)


def split(x):
    high = x.astype(BF16)
    return high, (x - high.astype(F32)).astype(BF16)


def mm(a, b, dims=((1,), (0,))):
    return lax.dot_general(a, b, (dims, ((), ())), preferred_element_type=F32)


def mm3(a, high, low):
    a_high, a_low = split(a)
    return mm(a_high, high) + (mm(a_low, high) + mm(a_high, low))


def correlate_kernel(
    span, walk_ref, ids_ref, s_ref, e_ref, swap_ref, pick_ref, out_ref,
    lhs_ref, rhs_ref, diag_ref, send, got, send_sem, recv_sem,
):
    block = pl.program_id(0)
    chunks = s_ref.shape[1] // CHUNK
    devices, rows_sent = out_ref.shape[0], out_ref.shape[1]
    blocks = out_ref.shape[2] // 2
    me = lax.axis_index("tm")
    barrier = pltpu.get_barrier_semaphore()
    peers = [lax.rem(me + k, devices) for k in range(1, devices)]

    @pl.when(block == 0)
    def _():
        for peer in peers:
            pl.semaphore_signal(barrier, inc=1, device_id={"tm": peer}, device_id_type=MESH)
        send[...] = jnp.zeros_like(send)

    swap = swap_ref[...]
    for ch in range(chunks):
        at = ch * CHUNK
        turned = mm(s_ref[0, at : at + CHUNK, :], swap, ((0,), (0,)))
        lhs_ref[:, at : at + CHUNK] = turned.astype(BF16)
        late = at + SEG_ROWS
        rhs_ref[ch, CHUNK:, :] = mm(swap, e_ref[0, late : late + CHUNK, :]).astype(BF16)
        rhs_ref[ch, :CHUNK, :] = mm(swap, e_ref[0, at : at + CHUNK, :]).astype(BF16)

    def product(a):
        off = (SEG_ROWS - a) * SEG_ROWS
        rhs = jnp.concatenate([rhs_ref[ch, off : off + CHUNK, :] for ch in range(chunks)], 0)
        g = mm(lhs_ref[...], rhs)
        return (
            g[:LANES, :LANES] + g[LANES:, LANES:],
            g[LANES:, :LANES] - g[:LANES, LANES:],
        )

    lower = iota((LANES, LANES), 1) <= iota((LANES, LANES), 0)
    later = product(SEG_ROWS)
    for a in reversed(range(SEG_ROWS)):
        here = product(a)
        for part in range(2):
            x = jnp.where(lower, here[part], later[part])
            half = LANES // 2
            while half >= 8:
                x = x[:half] + pltpu.roll(x[half:], LANES - half, 1)
                half //= 2
            diag_ref[part, a] = x
        later = here

    x = diag_ref[...].reshape(2 * SEG_ROWS * 8, LANES)
    sub = iota(x.shape, 0)
    for bit in (4, 2, 1):
        x = jnp.where((sub & bit) != 0, pltpu.roll(x, LANES - bit, 1), x)
    high, low = split(x)
    x = mm(pick_ref[...], high) + mm(pick_ref[...], low)
    shift = walk_ref[block] + REACH
    place = iota((LANES, LANES), 0) + iota((LANES, LANES), 1) - shift
    turn = jnp.where((place & (LANES - 1)) == 0, 1.0, 0.0).astype(BF16)
    high = x.astype(BF16)
    mid, low = split(x - high.astype(F32))
    x = mm(high, turn) + (mm(mid, turn) + mm(low, turn))
    lane = iota((SEG_ROWS, LANES), 1)
    label = jnp.full((1, LANES), ids_ref[block], jnp.int32).astype(F32)
    zero = jnp.zeros((1, LANES), F32)
    for part in range(2):
        own = x[part * SEG_ROWS : (part + 1) * SEG_ROWS]
        above = jnp.concatenate([zero, own[: SEG_ROWS - 1]], 0)
        tail = jnp.where(lane[:1] < REACH, own[SEG_ROWS - 1 :], 0.0)
        own = jnp.where(lane < shift, above, own)
        slot = 2 * block + part
        for dev in range(devices):
            first = dev * span // LANES
            for r in range(rows_sent):
                at = first + r
                row = own[at : at + 1] if at < SEG_ROWS else tail if at == SEG_ROWS else zero
                if r == rows_sent - 1:
                    row = jnp.where(lane[:1] == LANES - 1, label, row)
                send[dev, r, pl.ds(slot, 1), :] = row

    @pl.when(block == blocks - 1)
    def _():
        pl.semaphore_wait(barrier, devices - 1)
        copies = []
        for k, peer in enumerate(peers):
            copy = pltpu.make_async_remote_copy(
                src_ref=send.at[peer],
                dst_ref=got.at[me],
                send_sem=send_sem.at[k],
                recv_sem=recv_sem.at[k],
                device_id={"tm": peer},
                device_id_type=MESH,
            )
            copy.start()
            copies.append(copy)
        got[me] = send[me]
        for copy in copies:
            copy.wait()
        out_ref[...] = got[...]


def cosine(count):
    wrapped = ((count + DOP // 2) & (DOP - 1)) - DOP // 2
    z = (DOP // 4 - jnp.abs(wrapped)).astype(F32) * (2.0 * math.pi / DOP)
    z2 = z * z
    poly = -1.0 / 39916800.0
    for c in (1.0 / 362880.0, -1.0 / 5040.0, 1.0 / 120.0, -1.0 / 6.0, 1.0):
        poly = poly * z2 + c
    return z * poly


def map_kernel(
    span, got, guard_ref, size_ref, dft_high, dft_low, tab_high, tab_low, ker_high, ker_low,
    out_ref, power_ref, coef_ref,
):
    me = lax.axis_index("tm")
    devices, rows_sent, per = got.shape[:3]
    total = devices * per // 2
    if span % LANES == 0:
        lead, width = REACH, span + 2 * REACH
    else:
        width = rows_sent * LANES
        lead = pl.multiple_of(lax.rem(me * span, LANES) + REACH, 8)
    guard = guard_ref[...].astype(F32)
    size = size_ref[...].astype(F32)
    guard = jnp.transpose(jnp.broadcast_to(guard, (LANES, span)))
    outer = guard + jnp.transpose(jnp.broadcast_to(size, (LANES, span)))
    dist = iota((span, LANES), 1).astype(F32)
    inside = jnp.where((dist > guard) & (dist <= outer), 1.0, 0.0).astype(BF16)
    kernel = mm(inside, ker_high[...]) + mm(inside, ker_low[...])
    guard, outer = guard[:, :1], outer[:, :1]
    dist = jnp.abs(iota((span, width), 1) - lead - iota((span, width), 0)).astype(F32)
    band = jnp.where((dist > guard) & (dist <= outer), 1.0, 0.0).astype(BF16)
    spot = (me * span + iota((span, 1), 0)).astype(F32)
    last = (D - 1) - spot
    count = jnp.minimum(spot, outer) - jnp.minimum(spot, guard)
    count = count + jnp.minimum(last, outer) - jnp.minimum(last, guard)
    weight = 1.0 / (count + 2.0 * (outer - guard))

    rows = [[got[dev, r] for r in range(rows_sent)] for dev in range(devices)]
    stacked = jnp.concatenate([jnp.concatenate(r, 1) for r in rows], 0)
    ids = stacked[:, rows_sent * LANES - 1 :].astype(jnp.int32)
    shape = (devices * per, DOP)
    turns = ids * iota(shape, 1) - (DOP // 4) * (iota(shape, 0) & 1)
    mix_re_high, mix_re_low = split(cosine(turns))
    mix_im_high, mix_im_low = split(cosine(turns + DOP // 4))
    corr = jnp.transpose(stacked)[:width]
    corr_high, corr_low = split(corr)
    norm = 1.0 / (total * SEGS * D)
    re = mm(corr_high, mix_re_high) + (mm(corr_low, mix_re_high) + mm(corr_high, mix_re_low))
    im = mm(corr_high, mix_im_high) + (mm(corr_low, mix_im_high) + mm(corr_high, mix_im_low))
    power = (re * re + im * im) * norm
    floor = jnp.sum(corr * corr, axis=1, keepdims=True) * norm
    coef = mm3(power, dft_high[...], dft_low[...])
    if span % LANES == 0:
        power_c = power[lead : lead + span]
        coef_c = coef[lead : lead + span]
        floor_c = floor[lead : lead + span]
    else:
        power_ref[:, :DOP] = power
        power_ref[:, DOP:] = jnp.broadcast_to(floor, (width, LANES))
        coef_ref[...] = coef
        power_c = power_ref[pl.ds(lead, span), :DOP]
        floor_c = power_ref[pl.ds(lead, span), DOP:][:, :1]
        coef_c = coef_ref[pl.ds(lead, span), :]
    coef_high, coef_low = split(coef)
    sums = mm(band, coef_high) + mm(band, coef_low) + coef_c * kernel
    noise = mm3(sums, tab_high[...], tab_low[...]) * weight
    out_ref[...] = (power_c - floor_c) / (0.25 + noise)


def np_split(x):
    high = x.astype(BF16)
    return jnp.asarray(high), jnp.asarray((x - high.astype(np.float64)).astype(BF16))


def tables(total):
    lag, freq = np.arange(total), np.arange(DOP)
    angle = 2.0 * np.pi / DOP * ((lag[:, None] * freq[None, :]) % DOP)
    tab = np.concatenate([np.cos(angle), np.sin(angle)], 0)
    scale = np.where(lag == 0, 1.0, 2.0) / DOP
    dft = tab.T * np.concatenate([scale, scale])[None, :]
    dist = np.arange(LANES)
    ker = 2.0 * np.cos(2.0 * np.pi / DOP * ((dist[:, None] * lag[None, :]) % DOP))
    ker = np.concatenate([ker, ker], 1)
    return (*np_split(dft), *np_split(tab), *np_split(ker))


def body(surveillance, ref_samples, block_ids, walk, cfar_guard, cfar_window):
    blocks, rows_all = surveillance.shape[:2]
    devices = lax.axis_size("tm")
    total = blocks * devices
    span = D // devices
    rows_sent = window_rows(span)
    chunks = rows_all // CHUNK
    send_shape = (devices, rows_sent, 2 * blocks, LANES)
    smem = pl.BlockSpec(memory_space=pltpu.SMEM)
    vmem = pl.BlockSpec(memory_space=pltpu.VMEM)
    place = np.arange(CHUNK)
    swap = place[None, :] == (place % SEG_ROWS * SEG_ROWS + place // SEG_ROWS)[:, None]
    pick = np.arange(2 * SEG_ROWS)[:, None] == (np.arange(16 * SEG_ROWS) // 8)[None, :]
    windows = pl.pallas_call(
        functools.partial(correlate_kernel, span),
        grid=(blocks,),
        out_shape=jax.ShapeDtypeStruct(send_shape, F32),
        in_specs=[
            smem,
            smem,
            pl.BlockSpec((1,) + surveillance.shape[1:], lambda j: (j, 0, 0)),
            pl.BlockSpec((1,) + ref_samples.shape[1:], lambda j: (j, 0, 0)),
            vmem,
            vmem,
        ],
        out_specs=vmem,
        scratch_shapes=[
            pltpu.VMEM((2 * LANES, rows_all), BF16),
            pltpu.VMEM((chunks, 2 * CHUNK, 2 * LANES), BF16),
            pltpu.VMEM((2, SEG_ROWS, 8, LANES), F32),
            pltpu.VMEM(send_shape, F32),
            pltpu.VMEM(send_shape, F32),
            pltpu.SemaphoreType.DMA((devices,)),
            pltpu.SemaphoreType.DMA((devices,)),
        ],
        compiler_params=pltpu.CompilerParams(
            dimension_semantics=("arbitrary",), collective_id=0, has_side_effects=True
        ),
        name="correlate",
    )(walk, block_ids, surveillance, ref_samples, jnp.asarray(swap.astype(BF16)), jnp.asarray(pick.astype(BF16)))
    width = span + 2 * REACH if span % LANES == 0 else rows_sent * LANES
    return pl.pallas_call(
        functools.partial(map_kernel, span),
        out_shape=jax.ShapeDtypeStruct((span, DOP), F32),
        in_specs=[vmem] * 9,
        out_specs=vmem,
        scratch_shapes=[
            pltpu.VMEM((width, DOP + LANES), F32),
            pltpu.VMEM((width, 2 * total), F32),
        ],
        name="map",
    )(windows, cfar_guard.reshape(1, span), cfar_window.reshape(1, span), *tables(total))


def solution(mesh):
    in_specs = (
        P(("chan", "tm"), None, None),
        P("tm", None, None),
        P("tm"),
        P("tm"),
        P("tm"),
        P("tm"),
    )
    out_specs = P(("chan", "tm"), None)
    return jax.shard_map(body, mesh=mesh, in_specs=in_specs, out_specs=out_specs, check_vma=False)
```

time: 41.8 us -> 29.8 us (0.71)
  Pallas kernels: 38.4 us -> 29.6 us
  local copies, waits for them, and re-layouts: 1.87 us -> 0 us
  other arithmetic: 1.29 us -> 0 us
    pallas_call x1, Pallas kernels: 13.8 us -> 4.18 us  [body(): pl.pallas_call(functools.partial(map_kernel, span), out_shape=jax.ShapeDt...]
    unnamed x1 -> x0, local copies, waits for them, and re-layouts: 1.87 us -> none
    another operation x1 -> x0, other arithmetic: 1.29 us -> none  [body(): cfar = jnp.stack([cfar_guard, cfar_window])]
    pallas_call x1, Pallas kernels: 24.6 us -> 25.4 us  [body(): pl.pallas_call(functools.partial(correlate_kernel, span), grid=(blocks,),...]
where the time goes in v2:
time: 29.8 us; the launch traced here: 29.6 us
  Pallas kernels  29.6 us (99%)
    pallas_call x1, Pallas kernels, body(): pl.pallas_call(functools.partial(correlate_kernel, span), grid=(blocks,),...  25.4 us
    pallas_call x1, Pallas kernels, body(): pl.pallas_call(functools.partial(map_kernel, span), out_shape=jax.ShapeDt...  4.18 us

profile of v2, /device:TPU:0, one launch (start us, length us, event | category | flops | bytes accessed | tf_op | source)
XLA Modules:
  0.0 29.6 jit_solution(15702251230462859899)
XLA Ops:
  0.0 25.4 %correlate.1.got = f32[8,3,8,128]{3,2,1,0:T(8,128)} custom-call(s32[4]{0:T(128)} %walk_ref.1, s32[4]{0:T(128)} %ids_ref.1, bf16[4,1024,256]{2,1,0:T(8,128)(2,1)} %s_ref.1, bf16[4,1040,256]{2,1,0:T(8,128)(2,1)} %e_ref.1, bf16[256,256]{1,0:T(8,128)(2,1)} %constant.16.clone.swap_ref, bf16[32,256]{1,0:T(8,128)(2,1)} %constant.17.clone.pick_ref), custom_call_target="tpu_custom_call" | custom-call | tf_op jit(solution)/shard_map/correlate/pallas_call | solution.py:248
  25.4 4.2 %map.1 = f32[256,512]{1,0:T(8,128)} custom-call(f32[8,3,8,128]{3,2,1,0:T(8,128)} %correlate.1.got, s32[1,256]{1,0:T(1,128)} %bitcast.2, s32[1,256]{1,0:T(1,128)} %bitcast.3, bf16[512,64]{1,0:T(8,128)(2,1)} %constant.18.clone.dft_high, bf16[512,64]{1,0:T(8,128)(2,1)} %constant.19.clone.dft_low, bf16[64,512]{1,0:T(8,128)(2,1)} %constant.20.clone.tab_high, ...), custom_call_target="tpu_custom_call" | custom-call | tf_op jit(solution)/shard_map/map/pallas_call | solution.py:276

commit v3 on v2

--- a/solution.py
+++ b/solution.py
@@ -61,7 +61,40 @@
     def _():
         for peer in peers:
             pl.semaphore_signal(barrier, inc=1, device_id={"tm": peer}, device_id_type=MESH)
-        send[...] = jnp.zeros_like(send)
+        diag_ref[...] = jnp.zeros_like(diag_ref)
+
+    def finish(done):
+        x = diag_ref[...].reshape(2 * SEG_ROWS * 8, LANES)
+        sub = iota(x.shape, 0)
+        for bit in (4, 2, 1):
+            x = jnp.where((sub & bit) != 0, pltpu.roll(x, LANES - bit, 1), x)
+        high, low = split(x)
+        x = mm(pick_ref[...], high) + mm(pick_ref[...], low)
+        shift = walk_ref[done] + REACH
+        place = iota((LANES, LANES), 0) + iota((LANES, LANES), 1) - shift
+        turn = jnp.where((place & (LANES - 1)) == 0, 1.0, 0.0).astype(BF16)
+        high = x.astype(BF16)
+        mid, low = split(x - high.astype(F32))
+        x = mm(high, turn) + (mm(mid, turn) + mm(low, turn))
+        lane = iota((SEG_ROWS, LANES), 1)
+        label = jnp.full((1, LANES), ids_ref[done], jnp.int32).astype(F32)
+        zero = jnp.zeros((1, LANES), F32)
+        for part in range(2):
+            own = x[part * SEG_ROWS : (part + 1) * SEG_ROWS]
+            above = jnp.concatenate([zero, own[: SEG_ROWS - 1]], 0)
+            tail = jnp.where(lane[:1] < REACH, own[SEG_ROWS - 1 :], 0.0)
+            own = jnp.where(lane < shift, above, own)
+            slot = 2 * done + part
+            for dev in range(devices):
+                first = dev * span // LANES
+                for r in range(rows_sent):
+                    at = first + r
+                    row = own[at : at + 1] if at < SEG_ROWS else tail if at == SEG_ROWS else zero
+                    if r == rows_sent - 1:
+                        row = jnp.where(lane[:1] == LANES - 1, label, row)
+                    send[dev, r, pl.ds(slot, 1), :] = row
+
+    finish(jnp.maximum(block - 1, 0))
 
     swap = swap_ref[...]
     for ch in range(chunks):
@@ -94,38 +127,9 @@
             diag_ref[part, a] = x
         later = here
 
-    x = diag_ref[...].reshape(2 * SEG_ROWS * 8, LANES)
-    sub = iota(x.shape, 0)
-    for bit in (4, 2, 1):
-        x = jnp.where((sub & bit) != 0, pltpu.roll(x, LANES - bit, 1), x)
-    high, low = split(x)
-    x = mm(pick_ref[...], high) + mm(pick_ref[...], low)
-    shift = walk_ref[block] + REACH
-    place = iota((LANES, LANES), 0) + iota((LANES, LANES), 1) - shift
-    turn = jnp.where((place & (LANES - 1)) == 0, 1.0, 0.0).astype(BF16)
-    high = x.astype(BF16)
-    mid, low = split(x - high.astype(F32))
-    x = mm(high, turn) + (mm(mid, turn) + mm(low, turn))
-    lane = iota((SEG_ROWS, LANES), 1)
-    label = jnp.full((1, LANES), ids_ref[block], jnp.int32).astype(F32)
-    zero = jnp.zeros((1, LANES), F32)
-    for part in range(2):
-        own = x[part * SEG_ROWS : (part + 1) * SEG_ROWS]
-        above = jnp.concatenate([zero, own[: SEG_ROWS - 1]], 0)
-        tail = jnp.where(lane[:1] < REACH, own[SEG_ROWS - 1 :], 0.0)
-        own = jnp.where(lane < shift, above, own)
-        slot = 2 * block + part
-        for dev in range(devices):
-            first = dev * span // LANES
-            for r in range(rows_sent):
-                at = first + r
-                row = own[at : at + 1] if at < SEG_ROWS else tail if at == SEG_ROWS else zero
-                if r == rows_sent - 1:
-                    row = jnp.where(lane[:1] == LANES - 1, label, row)
-                send[dev, r, pl.ds(slot, 1), :] = row
-
     @pl.when(block == blocks - 1)
     def _():
+        finish(block)
         pl.semaphore_wait(barrier, devices - 1)
         copies = []
         for k, peer in enumerate(peers):

time: 29.8 us -> 29.6 us (level)
  no operation moved by 1% of the time
where the time goes in v3:
time: 29.6 us; the launch traced here: 29.4 us
  Pallas kernels  29.4 us (99%)
    pallas_call x1, Pallas kernels, body(): pl.pallas_call(functools.partial(correlate_kernel, span), grid=(blocks,),...  25.2 us
    pallas_call x1, Pallas kernels, body(): pl.pallas_call(functools.partial(map_kernel, span), out_shape=jax.ShapeDt...  4.18 us

profile of v3, /device:TPU:0, one launch (start us, length us, event | category | flops | bytes accessed | tf_op | source)
XLA Modules:
  0.0 29.4 jit_solution(13047411214618618992)
XLA Ops:
  0.0 25.2 %correlate.1.got = f32[8,3,8,128]{3,2,1,0:T(8,128)} custom-call(s32[4]{0:T(128)} %walk_ref.1, s32[4]{0:T(128)} %ids_ref.1, bf16[4,1024,256]{2,1,0:T(8,128)(2,1)} %s_ref.1, bf16[4,1040,256]{2,1,0:T(8,128)(2,1)} %e_ref.1, bf16[256,256]{1,0:T(8,128)(2,1)} %constant.16.clone.swap_ref, bf16[32,256]{1,0:T(8,128)(2,1)} %constant.17.clone.pick_ref), custom_call_target="tpu_custom_call" | custom-call | tf_op jit(solution)/shard_map/correlate/pallas_call | solution.py:252
  25.2 4.2 %map.1 = f32[256,512]{1,0:T(8,128)} custom-call(f32[8,3,8,128]{3,2,1,0:T(8,128)} %correlate.1.got, s32[1,256]{1,0:T(1,128)} %bitcast.2, s32[1,256]{1,0:T(1,128)} %bitcast.3, bf16[512,64]{1,0:T(8,128)(2,1)} %constant.18.clone.dft_high, bf16[512,64]{1,0:T(8,128)(2,1)} %constant.19.clone.dft_low, bf16[64,512]{1,0:T(8,128)(2,1)} %constant.20.clone.tab_high, ...), custom_call_target="tpu_custom_call" | custom-call | tf_op jit(solution)/shard_map/map/pallas_call | solution.py:280
